TPU v7x, 256 devices: a whole 4x4x8 slice. The times are simulated.
256 devices in a mesh: blk: 32 (over z_lo, x, core), grp: 8 (over z_hi, y).
Axes of the slice: x: 4, y: 4, z: 8 (z_hi: 2, z_lo: 4; z = z_hi * 4 + z_lo), core: 2. Of those that a mesh axis runs over, the one named last changes fastest.
Arguments:
- lambda_init: float32 [131072, 256], P('blk'), may hold values from 0.1 to 200
- gamma_init: float32 [32768, 256], P(('blk', 'grp')), may hold values from 0.5 to 20
- dmr_table: float32 [1024, 256], replicated, may hold values from -3 to 3
- features: int32 [32768, 4], P(('blk', 'grp')), may hold values from 0 to 1023
- counts: int32 [256, 4, 6, 128, 128], P(('blk', 'grp')), may hold values from 0 to 3
- tile_cols: int32 [256, 4, 6], P(('blk', 'grp')), may hold values from 0 to 31, as said below
- live_slots: int32 [256, 4], P(('blk', 'grp')), may hold values from 1 to 6, as said below
Outputs:
- gamma_out: float32 [32768, 256], P(('blk', 'grp'))
- lambda_out: float32 [131072, 256], P(('blk', 'grp'))
Inputs may be any that keep to these rules, and one draw needn't show every extreme that they name: `tile_cols`: within one row tile and substep the 6 column tiles are distinct. Slots 0 to live_slots - 1 of a row tile and substep are in use, the others are padding; row tile 0 uses all 6 slots in substep 0.
All inputs are finite; a program needn't handle non-finite values.
Results may differ from a plain program's by a relative error of at most 0.009.
Values sent between devices are 32-bit elements; how exact they have to be, the bound alone decides.
A program may use at most 128 MiB of HBM per device.

v0:
```python
import jax
import jax.numpy as jnp
from jax import lax
from jax.sharding import PartitionSpec as P

STRATA = 4
LOCAL = 3
pass_bits = (0, 1, 0)
step_weight = 0.5
word_prior = 0.05


def partner(value, axis, bit):
    mask = 2**bit
    pairs = [(source, source ^ mask) for source in range(lax.axis_size(axis))]
    return lax.ppermute(value, axis, pairs)


def expected_theta(doc_gamma):
    return jnp.exp(
        lax.digamma(doc_gamma) - lax.digamma(jnp.sum(doc_gamma, axis=1, keepdims=True))
    ).astype(jnp.bfloat16)


def update_padded(doc_gamma, doc_alpha, beta_exp, tile_counts, column_ids, live_count):
    rows, slots = column_ids.shape
    tile = tile_counts.shape[-1]
    topics = beta_exp.shape[1]
    columns = beta_exp.shape[0] // tile
    word_tiles = beta_exp.reshape(columns, tile, topics)[column_ids]
    active = jnp.arange(slots)[None, :] < live_count[:, None]
    tile_weight = jnp.where(active[:, :, None, None], tile_counts, 0).astype(jnp.float32)

    def ratio_of(theta_exp):
        theta_rows = theta_exp.reshape(rows, tile, topics)
        denom_tiles = jnp.einsum(
            "rdk,rswk->rsdw", theta_rows, word_tiles, preferred_element_type=jnp.float32
        )
        return (theta_rows, (tile_weight / denom_tiles).astype(jnp.bfloat16))

    for repeat in range(LOCAL):
        theta_exp = expected_theta(doc_gamma)
        theta_rows, count_ratio = ratio_of(theta_exp)
        contrib = jnp.einsum(
            "rsdw,rswk->rdk", count_ratio, word_tiles, preferred_element_type=jnp.float32
        )
        doc_gamma = doc_alpha + theta_exp.astype(jnp.float32) * contrib.reshape(doc_gamma.shape)
    theta_exp = expected_theta(doc_gamma)
    theta_rows, count_ratio = ratio_of(theta_exp)
    stat_tiles = jnp.einsum(
        "rsdw,rdk->rswk", count_ratio, theta_rows, preferred_element_type=jnp.float32
    )
    selector = (column_ids.reshape(-1)[None, :] == jnp.arange(columns)[:, None]).astype(jnp.float32)
    accumulated = jnp.dot(
        selector,
        stat_tiles.reshape(rows * slots, tile * topics),
        precision=lax.Precision.HIGHEST,
        preferred_element_type=jnp.float32,
    )
    partial_value = (beta_exp.astype(jnp.float32) * accumulated.reshape(beta_exp.shape)).astype(
        jnp.bfloat16
    )
    return (doc_gamma, partial_value)


def on_device(lambda_init, gamma_init, dmr_table, features, counts, tile_cols, live_slots):
    groups = lax.axis_size("grp")
    doc_alpha = jnp.exp(jnp.sum(jnp.take(dmr_table, features, axis=0), axis=1))
    topic_panel = lambda_init
    doc_gamma = gamma_init
    ahead = [(counts[:, step], tile_cols[:, step], live_slots[:, step]) for step in range(STRATA)]
    for substep in range(STRATA):
        topic_totals = lax.psum(jnp.sum(topic_panel, axis=0), "blk")
        beta_exp = jnp.exp(lax.digamma(topic_panel) - lax.digamma(topic_totals)[None, :]).astype(
            jnp.bfloat16
        )
        tile_counts, column_ids, live_count = ahead[substep]
        doc_gamma, partial_value = update_padded(
            doc_gamma, doc_alpha, beta_exp, tile_counts, column_ids, live_count
        )
        partial_wide = partial_value.astype(jnp.float32)
        topic_panel = (1.0 - step_weight) * topic_panel + step_weight * (
            word_prior + groups * partial_wide
        )
        if substep + 1 < STRATA:
            topic_panel = partner(topic_panel, "blk", pass_bits[substep])
    returned = partner(topic_panel, "blk", 1)
    lambda_out = lax.psum_scatter(returned, "grp", scatter_dimension=0, tiled=True) / groups
    return (doc_gamma, lambda_out)


def solution(mesh):
    placed = (
        P("blk", None),
        P(("blk", "grp"), None),
        P(),
        P(("blk", "grp"), None),
        P(("blk", "grp"), None, None, None, None),
        P(("blk", "grp"), None, None),
        P(("blk", "grp"), None),
    )
    return jax.shard_map(
        on_device,
        mesh=mesh,
        in_specs=placed,
        out_specs=(P(("blk", "grp"), None), P(("blk", "grp"), None)),
        check_vma=False,
    )
```

profile of v0, /device:TPU:2, one launch (start us, length us, event | category | flops | bytes accessed | tf_op | source)
XLA Modules:
  0.0 971.4 jit_solution(11349944712622576817)
XLA Ops:
  14.2 2.7 reduce_sum.176
  17.0 68.1 %psum.28 = f32[256]{0:T(256)S(1)} all-reduce(f32[256]{0:T(256)S(1)} %reduce_sum.176), channel_id=1, replica_groups=mesh['blk'=32,'grp'=8] {'blk'}, use_global_device_ids=true, to_apply=%region_3.4 | all-reduce | flops 256 | bytes 2048 | tf_op jit(solution)/shard_map/psum | solution.py:73
  85.2 31.2 %fusion.4 = bf16[4096,256]{1,0:T(8,128)(2,1)} fusion(f32[4096,256]{1,0:T(8,128)} %param.7, f32[256]{0:T(256)S(1)} %compare_select_fusion.20), kind=kLoop, calls=%fused_computation.17 | loop fusion | flops 80740352 | bytes 6292480 | tf_op jit(solution)/shard_map/convert_element_type | solution.py:74
  124.1 2.3 fusion.1346
  131.5 3.7 fusion.796
  135.2 4.9 reshape.2574
  140.1 33.2 %add_multiply_fusion.3 = f32[4096,256]{1,0:T(8,128)} fusion(f32[4096,256]{1,0:T(8,128)} %param.7, f32[4096,256]{1,0:T(8,128)} %reshape.2574, f32[256]{0:T(256)S(1)} %copy-done.7), kind=kLoop, calls=%fused_computation.39 | loop fusion | flops 89128960 | bytes 12583936 | tf_op jit(solution)/shard_map/add | solution.py:82
  174.3 6.7 collective-permute-done
  180.9 2.7 reduce_sum.180
  183.7 67.9 %psum.29 = f32[256]{0:T(256)S(1)} all-reduce(f32[256]{0:T(256)S(1)} %reduce_sum.180), channel_id=1, replica_groups=mesh['blk'=32,'grp'=8] {'blk'}, use_global_device_ids=true, to_apply=%region_8.9 | all-reduce | flops 256 | bytes 2048 | tf_op jit(solution)/shard_map/psum | solution.py:73
  251.6 31.1 %fusion.9 = bf16[4096,256]{1,0:T(8,128)(2,1)} fusion(f32[4096,256]{1,0:T(8,128)} %collective-permute-done, f32[256]{0:T(256)S(1)} %compare_select_fusion.16), kind=kLoop, calls=%fused_computation.22 | loop fusion | flops 80740352 | bytes 6292480 | tf_op jit(solution)/shard_map/convert_element_type | solution.py:74
  292.9 3.7 fusion.797
  296.6 4.9 reshape.2582
  301.5 33.2 %add_multiply_fusion.2 = f32[4096,256]{1,0:T(8,128)} fusion(f32[4096,256]{1,0:T(8,128)} %collective-permute-done, f32[4096,256]{1,0:T(8,128)} %reshape.2582, f32[256]{0:T(256)S(1)} %compare_select_fusion.16), kind=kLoop, calls=%fused_computation.37 | loop fusion | flops 89128960 | bytes 12583936 | tf_op jit(solution)/shard_map/add | solution.py:82
  334.7 6.4 collective-permute-start.1
  342.0 90.0 %collective-permute-done.1 = f32[4096,256]{1,0:T(8,128)} collective-permute-done((f32[4096,256]{1,0:T(8,128)}, f32[4096,256]{1,0:T(8,128)}, u32[]{:S(2)}, u32[]{:S(2)}) %collective-permute-start.1) | collective-permute-done | bytes 4194336 | tf_op jit(solution)/shard_map/ppermute | solution.py:16
  431.9 2.7 reduce_sum.184
  434.7 62.9 %psum.30 = f32[256]{0:T(256)S(1)} all-reduce(f32[256]{0:T(256)S(1)} %reduce_sum.184), channel_id=1, replica_groups=mesh['blk'=32,'grp'=8] {'blk'}, use_global_device_ids=true, to_apply=%region_13.14 | all-reduce | flops 256 | bytes 2048 | tf_op jit(solution)/shard_map/psum | solution.py:73
  497.7 31.1 %fusion.14 = bf16[4096,256]{1,0:T(8,128)(2,1)} fusion(f32[4096,256]{1,0:T(8,128)} %collective-permute-done.1, f32[256]{0:T(256)S(1)} %compare_select_fusion.12), kind=kLoop, calls=%fused_computation.27 | loop fusion | flops 80740352 | bytes 6292480 | tf_op jit(solution)/shard_map/convert_element_type | solution.py:74
  538.3 3.7 fusion.798
  542.1 4.9 reshape.2590
  546.9 33.2 %add_multiply_fusion.1 = f32[4096,256]{1,0:T(8,128)} fusion(f32[4096,256]{1,0:T(8,128)} %collective-permute-done.1, f32[4096,256]{1,0:T(8,128)} %reshape.2590, f32[256]{0:T(256)S(1)} %compare_select_fusion.12), kind=kLoop, calls=%fused_computation.35 | loop fusion | flops 89128960 | bytes 12583936 | tf_op jit(solution)/shard_map/add | solution.py:82
  581.3 6.7 collective-permute-done.2
  587.9 2.7 reduce_sum.188
  590.7 67.5 %psum.31 = f32[256]{0:T(256)S(1)} all-reduce(f32[256]{0:T(256)S(1)} %reduce_sum.188), channel_id=1, replica_groups=mesh['blk'=32,'grp'=8] {'blk'}, use_global_device_ids=true, to_apply=%region_18.19 | all-reduce | flops 256 | bytes 2048 | tf_op jit(solution)/shard_map/psum | solution.py:73
  658.2 31.0 %fusion.19 = bf16[4096,256]{1,0:T(8,128)(2,1)} fusion(f32[4096,256]{1,0:T(8,128)} %collective-permute-done.2, f32[256]{0:T(256)S(1)} %compare_select_fusion.8), kind=kLoop, calls=%fused_computation.32 | loop fusion | flops 80740352 | bytes 6292480 | tf_op jit(solution)/shard_map/convert_element_type | solution.py:74
  699.6 3.7 fusion.799
  703.4 4.9 reshape.2598
  708.3 31.3 %add_multiply_fusion = f32[4096,256]{1,0:T(8,128)S(1)} fusion(f32[4096,256]{1,0:T(8,128)} %collective-permute-done.2, f32[4096,256]{1,0:T(8,128)} %reshape.2598, f32[256]{0:T(256)S(1)} %compare_select_fusion.8), kind=kLoop, calls=%fused_computation.33 | loop fusion | flops 89128960 | bytes 12583936 | tf_op jit(solution)/shard_map/add | solution.py:82
  739.6 6.3 collective-permute-start.3
  745.9 90.6 %collective-permute-done.3 = f32[4096,256]{1,0:T(8,128)} collective-permute-done((f32[4096,256]{1,0:T(8,128)S(1)}, f32[4096,256]{1,0:T(8,128)}, u32[]{:S(2)}, u32[]{:S(2)}) %collective-permute-start.3) | collective-permute-done | bytes 4194336 | tf_op jit(solution)/shard_map/ppermute | solution.py:16
  836.5 126.0 %reduce-scatter.2.cloned.1.call-done = f32[512,256]{1,0:T(8,128)} async-done(((f32[4096,256]{1,0:T(8,128)}), f32[512,256]{1,0:T(8,128)}) %reduce-scatter.2.cloned.1.call-update) | async-done | bytes 524304 | tf_op jit(solution)/shard_map/reduce_scatter | solution.py:88
  (114 shorter events, 54.5 us)
Async XLA Ops:
  7.2 4.6 copy-start
  7.2 955.3 %reduce-scatter.2.cloned.1.call-start = ((), (), s32[]{:S(2)}) async-start(), calls=%async_computation.1 | async-start | bytes 4718592 | tf_op jit(solution)/shard_map/reduce_scatter | solution.py:88
  17.0 99.4 %copy-start.2 = (s32[1,4,6,128,128]{4,3,2,1,0:T(8,128)S(1)}, s32[1,4,6,128,128]{4,3,2,1,0:T(8,128)}, u32[]{:S(2)}) copy-start(s32[1,4,6,128,128]{4,3,2,1,0:T(8,128)} %param.11) | copy-start | bytes 4718596
  85.2 32.1 %copy-start.6 = (f32[256]{0:T(256)}, f32[256]{0:T(256)S(1)}, u32[]{:S(2)}) copy-start(f32[256]{0:T(256)S(1)} %compare_select_fusion.20) | copy-start | bytes 3076
  85.2 32.3 %copy-start.5 = (s32[1,4]{1,0:T(1,128)S(1)}, s32[1,4]{1,0:T(1,128)}, u32[]{:S(2)}) copy-start(s32[1,4]{1,0:T(1,128)} %param.13) | copy-start | bytes 52
  85.2 33.7 %copy-start.4 = (f32[128,256]{1,0:T(8,128)S(1)}, f32[128,256]{1,0:T(8,128)}, u32[]{:S(2)}) copy-start(f32[128,256]{1,0:T(8,128)} %param.8) | copy-start | bytes 393220
  126.5 4.9 copy-start.14
  129.9 0.6 copy-start.18
  135.2 4.9 copy-start.7
  140.1 33.3 %copy-start.3 = (s32[1,1,6,128,128]{4,3,2,1,0:T(8,128)S(1)}, s32[1,1,6,128,128]{4,3,2,1,0:T(8,128)}, u32[]{:S(2)}) copy-start(s32[1,1,6,128,128]{4,3,2,1,0:T(8,128)} %get-tuple-element.4) | copy-start | bytes 1179652
  140.1 34.2 %copy-start.10 = (s32[6]{0:T(128)S(1)}, s32[6]{0:T(128)}, u32[]{:S(2)}) copy-start(s32[6]{0:T(128)} %get-tuple-element.11) | copy-start | bytes 76
  173.4 7.6 collective-permute-start
  251.6 33.2 %copy-start.19 = (bf16[128,256]{1,0:T(8,128)(2,1)S(1)}, bf16[128,256]{1,0:T(8,128)(2,1)}, u32[]{:S(2)}) copy-start(bf16[128,256]{1,0:T(8,128)(2,1)} %copy-done.18) | copy-start | bytes 196612
  287.9 5.0 copy-start.13
  291.3 0.6 copy-start.16
  301.5 40.4 %copy-start.9 = (s32[6]{0:T(128)S(1)}, s32[6]{0:T(128)}, u32[]{:S(2)}) copy-start(s32[6]{0:T(128)} %get-tuple-element.13) | copy-start | bytes 76
  334.7 97.2 %collective-permute-start.1 = (f32[4096,256]{1,0:T(8,128)}, f32[4096,256]{1,0:T(8,128)}, u32[]{:S(2)}, u32[]{:S(2)}) collective-permute-start(f32[4096,256]{1,0:T(8,128)} %add_multiply_fusion.2), channel_id=1, source_target_pairs={{0,16},{8,24},{16,0},{24,8},{32,48},{40,56},{48,32},{56,40},{64,80... | collective-permute-start | bytes 12582920 | tf_op jit(solution)/shard_map/ppermute | solution.py:16
  497.7 33.2 %copy-start.17 = (bf16[128,256]{1,0:T(8,128)(2,1)S(1)}, bf16[128,256]{1,0:T(8,128)(2,1)}, u32[]{:S(2)}) copy-start(bf16[128,256]{1,0:T(8,128)(2,1)} %copy-done.16) | copy-start | bytes 196612
  534.0 4.3 copy-start.12
  546.9 34.3 %copy-start.8 = (s32[6]{0:T(128)S(1)}, s32[6]{0:T(128)}, u32[]{:S(2)}) copy-start(s32[6]{0:T(128)} %get-tuple-element.10) | copy-start | bytes 76
  580.1 7.8 collective-permute-start.2
  696.8 2.3 copy-start.15
  696.9 2.7 copy-start.11
  708.3 256.0 %copy-start.1 = (f32[1024,256]{1,0:T(8,128)S(1)}, f32[1024,256]{1,0:T(8,128)}, u32[]{:S(2)}) copy-start(f32[1024,256]{1,0:T(8,128)} %param.9) | copy-start | bytes 3145732
  739.6 96.8 %collective-permute-start.3 = (f32[4096,256]{1,0:T(8,128)S(1)}, f32[4096,256]{1,0:T(8,128)}, u32[]{:S(2)}, u32[]{:S(2)}) collective-permute-start(f32[4096,256]{1,0:T(8,128)S(1)} %add_multiply_fusion), channel_id=1, source_target_pairs={{0,16},{8,24},{16,0},{24,8},{32,48},{40,56},{48,32},{56,40},{64,80... | collective-permute-start | bytes 12582920 | tf_op jit(solution)/shard_map/ppermute | solution.py:16
Sparse Core Ops, SparseCore 0:
  836.6 125.7 reduce-scatter.1
where the time goes:
time: 976 us; the launch traced here: 971 us
  waiting for transfers between devices  320 us (33%)
  other arithmetic  278 us (28%)
  blocking collectives  266 us (27%)
  matrix products  41.4 us (4%)
  local copies, waits for them, and re-layouts  37.3 us (4%)
  between operations  14.9 us (2%)
  starting transfers between devices  13.1 us (1%)
    psum x4, blocking collectives, on_device(): topic_totals = lax.psum(jnp.sum(topic_panel, axis=0), 'blk')  266 us
    ppermute x4, waiting for transfers between devices, partner(): return lax.ppermute(value, axis, pairs)  194 us
    add x4, other arithmetic, on_device(): (1.0 - step_weight) * topic_panel  131 us
    reduce_scatter x1, waiting for transfers between devices, on_device(): lax.psum_scatter(returned, 'grp', scatter_dimension=0, tiled=True) / groups  126 us
    convert_element_type x4, other arithmetic, on_device(): jnp.exp(lax.digamma(topic_panel) - lax.digamma(topic_totals)[None, :])  124 us
    dot_general x12, matrix products, update_padded(): jnp.einsum('rsdw,rswk->rdk', count_ratio, word_tiles, preferred_element_t...  22.8 us
    reshape x4, local copies, waits for them, and re-layouts, update_padded(): accumulated.reshape(beta_exp.shape)  19.6 us
  transfers between devices with their start and end apart: 5, of which 5 were waited for; matrix products, arithmetic and copies ran while one was open for 0% of the time, Pallas kernels for 0%

commit v1 on v0

--- a/solution.py
+++ b/solution.py
@@ -70,7 +70,7 @@
     doc_gamma = gamma_init
     ahead = [(counts[:, step], tile_cols[:, step], live_slots[:, step]) for step in range(STRATA)]
     for substep in range(STRATA):
-        topic_totals = lax.psum(jnp.sum(topic_panel, axis=0), "blk")
+        topic_totals = jnp.sum(lax.all_gather(jnp.sum(topic_panel, axis=0), "blk"), axis=0)
         beta_exp = jnp.exp(lax.digamma(topic_panel) - lax.digamma(topic_totals)[None, :]).astype(
             jnp.bfloat16
         )

time: 976 us -> 862 us (0.88)
  blocking collectives: 266 us -> 160 us
  starting transfers between devices: 13.1 us -> 1.88 us
    psum x4 -> x0, blocking collectives: 266 us -> none  [on_device(): topic_totals = lax.psum(jnp.sum(topic_panel, axis=0), 'blk')]
    all_gather x0 -> x4, blocking collectives: none -> 160 us  [on_device(): lax.all_gather(jnp.sum(topic_panel, axis=0), 'blk')]
    ppermute x4, starting transfers between devices: 13.1 us -> 1.84 us  [partner(): return lax.ppermute(value, axis, pairs)]
where the time goes in v1:
time: 862 us; the launch traced here: 857 us
  waiting for transfers between devices  323 us (37%)
  other arithmetic  279 us (32%)
  blocking collectives  160 us (19%)
  matrix products  41.4 us (5%)
  local copies, waits for them, and re-layouts  37.3 us (4%)
  between operations  14.9 us (2%)
    ppermute x4, waiting for transfers between devices, partner(): return lax.ppermute(value, axis, pairs)  197 us
    all_gather x4, blocking collectives, on_device(): lax.all_gather(jnp.sum(topic_panel, axis=0), 'blk')  160 us
    add x4, other arithmetic, on_device(): (1.0 - step_weight) * topic_panel  131 us
    reduce_scatter x1, waiting for transfers between devices, on_device(): lax.psum_scatter(returned, 'grp', scatter_dimension=0, tiled=True) / groups  125 us
    convert_element_type x4, other arithmetic, on_device(): jnp.exp(lax.digamma(topic_panel) - lax.digamma(topic_totals)[None, :])  125 us
    dot_general x12, matrix products, update_padded(): jnp.einsum('rsdw,rswk->rdk', count_ratio, word_tiles, preferred_element_t...  22.8 us
    reshape x4, local copies, waits for them, and re-layouts, update_padded(): accumulated.reshape(beta_exp.shape)  19.6 us
  transfers between devices with their start and end apart: 5, of which 5 were waited for; matrix products, arithmetic and copies ran while one was open for 0% of the time, Pallas kernels for 0%

profile of v1, /device:TPU:2, one launch (start us, length us, event | category | flops | bytes accessed | tf_op | source)
XLA Modules:
  0.0 857.2 jit_solution(2237652085848487461)
XLA Ops:
  14.2 2.7 reduce_sum.212
  17.0 40.0 %all-gather.4 = f32[32,1,256]{2,1,0:T(1,128)S(1)} all-gather(f32[1,1,256]{2,1,0:T(1,128)S(1)} %bitcast.637), channel_id=2, replica_groups=mesh['blk'=32,'grp'=8] {'blk'}, dimensions={0}, use_global_device_ids=true | all-gather | bytes 33792 | tf_op jit(solution)/shard_map/all_gather | solution.py:73
  57.1 31.2 %fusion.4 = bf16[4096,256]{1,0:T(8,128)(2,1)} fusion(f32[4096,256]{1,0:T(8,128)} %param.7, f32[256]{0:T(256)S(1)} %compare_select_fusion.20), kind=kLoop, calls=%fused_computation.17 | loop fusion | flops 80740352 | bytes 6292480 | tf_op jit(solution)/shard_map/convert_element_type | solution.py:74
  98.5 2.3 fusion.1349
  103.4 3.7 fusion.796
  107.1 4.9 reshape.2890
  112.1 33.2 %add_multiply_fusion.3 = f32[4096,256]{1,0:T(8,128)} fusion(f32[4096,256]{1,0:T(8,128)} %param.7, f32[4096,256]{1,0:T(8,128)} %reshape.2890, f32[256]{0:T(256)S(1)} %copy-done.7), kind=kLoop, calls=%fused_computation.39 | loop fusion | flops 89128960 | bytes 12583936 | tf_op jit(solution)/shard_map/add | solution.py:82
  146.5 6.4 collective-permute-done
  152.9 2.7 reduce_sum.217
  155.6 42.6 %all-gather.5 = f32[32,1,256]{2,1,0:T(1,128)S(1)} all-gather(f32[1,1,256]{2,1,0:T(1,128)S(1)} %bitcast.638), channel_id=3, replica_groups=mesh['blk'=32,'grp'=8] {'blk'}, dimensions={0}, use_global_device_ids=true | all-gather | bytes 33792 | tf_op jit(solution)/shard_map/all_gather | solution.py:73
  198.4 31.4 %fusion.9 = bf16[4096,256]{1,0:T(8,128)(2,1)} fusion(f32[4096,256]{1,0:T(8,128)} %collective-permute-done, f32[256]{0:T(256)S(1)} %compare_select_fusion.16), kind=kLoop, calls=%fused_computation.22 | loop fusion | flops 80740352 | bytes 6292480 | tf_op jit(solution)/shard_map/convert_element_type | solution.py:74
  232.7 2.3 fusion.1355
  240.0 3.7 fusion.797
  243.8 4.9 reshape.2898
  248.7 33.2 %add_multiply_fusion.2 = f32[4096,256]{1,0:T(8,128)} fusion(f32[4096,256]{1,0:T(8,128)} %collective-permute-done, f32[4096,256]{1,0:T(8,128)} %reshape.2898, f32[256]{0:T(256)S(1)} %compare_select_fusion.16), kind=kLoop, calls=%fused_computation.37 | loop fusion | flops 89128960 | bytes 12583936 | tf_op jit(solution)/shard_map/add | solution.py:82
  283.1 92.0 %collective-permute-done.1 = f32[4096,256]{1,0:T(8,128)} collective-permute-done((f32[4096,256]{1,0:T(8,128)}, f32[4096,256]{1,0:T(8,128)}, u32[]{:S(2)}, u32[]{:S(2)}) %collective-permute-start.1) | collective-permute-done | bytes 4194336 | tf_op jit(solution)/shard_map/ppermute | solution.py:16
  375.0 2.7 reduce_sum.222
  377.8 38.1 %all-gather.6 = f32[32,1,256]{2,1,0:T(1,128)S(1)} all-gather(f32[1,1,256]{2,1,0:T(1,128)S(1)} %bitcast.639), channel_id=4, replica_groups=mesh['blk'=32,'grp'=8] {'blk'}, dimensions={0}, use_global_device_ids=true | all-gather | bytes 33792 | tf_op jit(solution)/shard_map/all_gather | solution.py:73
  416.0 31.1 %fusion.14 = bf16[4096,256]{1,0:T(8,128)(2,1)} fusion(f32[4096,256]{1,0:T(8,128)} %collective-permute-done.1, f32[256]{0:T(256)S(1)} %compare_select_fusion.12), kind=kLoop, calls=%fused_computation.27 | loop fusion | flops 80740352 | bytes 6292480 | tf_op jit(solution)/shard_map/convert_element_type | solution.py:74
  449.9 2.3 fusion.1364
  456.6 3.7 fusion.798
  460.4 4.9 reshape.2906
  465.2 33.2 %add_multiply_fusion.1 = f32[4096,256]{1,0:T(8,128)} fusion(f32[4096,256]{1,0:T(8,128)} %collective-permute-done.1, f32[4096,256]{1,0:T(8,128)} %reshape.2906, f32[256]{0:T(256)S(1)} %compare_select_fusion.12), kind=kLoop, calls=%fused_computation.35 | loop fusion | flops 89128960 | bytes 12583936 | tf_op jit(solution)/shard_map/add | solution.py:82
  499.9 6.4 collective-permute-done.2
  506.2 2.7 reduce_sum.227
  509.0 39.3 %all-gather.7 = f32[32,1,256]{2,1,0:T(1,128)S(1)} all-gather(f32[1,1,256]{2,1,0:T(1,128)S(1)} %bitcast.640), channel_id=5, replica_groups=mesh['blk'=32,'grp'=8] {'blk'}, dimensions={0}, use_global_device_ids=true | all-gather | bytes 33792 | tf_op jit(solution)/shard_map/all_gather | solution.py:73
  548.4 31.0 %fusion.19 = bf16[4096,256]{1,0:T(8,128)(2,1)} fusion(f32[4096,256]{1,0:T(8,128)} %collective-permute-done.2, f32[256]{0:T(256)S(1)} %compare_select_fusion.8), kind=kLoop, calls=%fused_computation.32 | loop fusion | flops 80740352 | bytes 6292480 | tf_op jit(solution)/shard_map/convert_element_type | solution.py:74
  589.8 3.7 fusion.799
  593.5 4.9 reshape.2914
  598.4 31.3 %add_multiply_fusion = f32[4096,256]{1,0:T(8,128)S(1)} fusion(f32[4096,256]{1,0:T(8,128)} %collective-permute-done.2, f32[4096,256]{1,0:T(8,128)} %reshape.2914, f32[256]{0:T(256)S(1)} %compare_select_fusion.8), kind=kLoop, calls=%fused_computation.33 | loop fusion | flops 89128960 | bytes 12583936 | tf_op jit(solution)/shard_map/add | solution.py:82
  630.2 92.6 %collective-permute-done.3 = f32[4096,256]{1,0:T(8,128)} collective-permute-done((f32[4096,256]{1,0:T(8,128)S(1)}, f32[4096,256]{1,0:T(8,128)}, u32[]{:S(2)}, u32[]{:S(2)}) %collective-permute-start.3) | collective-permute-done | bytes 4194336 | tf_op jit(solution)/shard_map/ppermute | solution.py:16
  722.8 125.4 %reduce-scatter.2.cloned.1.call-done = f32[512,256]{1,0:T(8,128)} async-done(((f32[4096,256]{1,0:T(8,128)}), f32[512,256]{1,0:T(8,128)}) %reduce-scatter.2.cloned.1.call-update) | async-done | bytes 524304 | tf_op jit(solution)/shard_map/reduce_scatter | solution.py:88
  (118 shorter events, 51.5 us)
Async XLA Ops:
  7.2 4.6 copy-start
  7.2 841.0 %reduce-scatter.2.cloned.1.call-start = ((), (), s32[]{:S(2)}) async-start(), calls=%async_computation.1 | async-start | bytes 4718592 | tf_op jit(solution)/shard_map/reduce_scatter | solution.py:88
  17.0 71.4 %copy-start.2 = (s32[1,4,6,128,128]{4,3,2,1,0:T(8,128)S(1)}, s32[1,4,6,128,128]{4,3,2,1,0:T(8,128)}, u32[]{:S(2)}) copy-start(s32[1,4,6,128,128]{4,3,2,1,0:T(8,128)} %param.11) | copy-start | bytes 4718596
  57.1 32.1 %copy-start.6 = (f32[256]{0:T(256)}, f32[256]{0:T(256)S(1)}, u32[]{:S(2)}) copy-start(f32[256]{0:T(256)S(1)} %compare_select_fusion.20) | copy-start | bytes 3076
  57.1 32.3 %copy-start.5 = (s32[1,4]{1,0:T(1,128)S(1)}, s32[1,4]{1,0:T(1,128)}, u32[]{:S(2)}) copy-start(s32[1,4]{1,0:T(1,128)} %param.13) | copy-start | bytes 52
  57.1 33.7 %copy-start.4 = (f32[128,256]{1,0:T(8,128)S(1)}, f32[128,256]{1,0:T(8,128)}, u32[]{:S(2)}) copy-start(f32[128,256]{1,0:T(8,128)} %param.8) | copy-start | bytes 393220
  98.5 5.0 copy-start.14
  101.8 0.6 copy-start.18
  107.1 4.9 copy-start.7
  112.1 33.6 %copy-start.3 = (s32[1,1,6,128,128]{4,3,2,1,0:T(8,128)S(1)}, s32[1,1,6,128,128]{4,3,2,1,0:T(8,128)}, u32[]{:S(2)}) copy-start(s32[1,1,6,128,128]{4,3,2,1,0:T(8,128)} %get-tuple-element.4) | copy-start | bytes 1179652
  112.1 34.4 %copy-start.10 = (s32[6]{0:T(128)S(1)}, s32[6]{0:T(128)}, u32[]{:S(2)}) copy-start(s32[6]{0:T(128)} %get-tuple-element.11) | copy-start | bytes 76
  145.3 7.6 collective-permute-start
  198.4 33.6 %copy-start.19 = (bf16[128,256]{1,0:T(8,128)(2,1)S(1)}, bf16[128,256]{1,0:T(8,128)(2,1)}, u32[]{:S(2)}) copy-start(bf16[128,256]{1,0:T(8,128)(2,1)} %copy-done.18) | copy-start | bytes 196612
  235.1 4.9 copy-start.13
  238.4 0.6 copy-start.16
  248.7 34.4 %copy-start.9 = (s32[6]{0:T(128)S(1)}, s32[6]{0:T(128)}, u32[]{:S(2)}) copy-start(s32[6]{0:T(128)} %get-tuple-element.13) | copy-start | bytes 76
  281.8 93.2 %collective-permute-start.1 = (f32[4096,256]{1,0:T(8,128)}, f32[4096,256]{1,0:T(8,128)}, u32[]{:S(2)}, u32[]{:S(2)}) collective-permute-start(f32[4096,256]{1,0:T(8,128)} %add_multiply_fusion.2), channel_id=1, source_target_pairs={{0,16},{8,24},{16,0},{24,8},{32,48},{40,56},{48,32},{56,40},{64,80... | collective-permute-start | bytes 12582920 | tf_op jit(solution)/shard_map/ppermute | solution.py:16
  416.0 33.2 %copy-start.17 = (bf16[128,256]{1,0:T(8,128)(2,1)S(1)}, bf16[128,256]{1,0:T(8,128)(2,1)}, u32[]{:S(2)}) copy-start(bf16[128,256]{1,0:T(8,128)(2,1)} %copy-done.16) | copy-start | bytes 196612
  452.3 4.3 copy-start.12
  465.2 34.6 %copy-start.8 = (s32[6]{0:T(128)S(1)}, s32[6]{0:T(128)}, u32[]{:S(2)}) copy-start(s32[6]{0:T(128)} %get-tuple-element.10) | copy-start | bytes 76
  498.4 7.8 collective-permute-start.2
  587.0 2.3 copy-start.15
  587.0 2.7 copy-start.11
  598.4 251.6 %copy-start.1 = (f32[1024,256]{1,0:T(8,128)S(1)}, f32[1024,256]{1,0:T(8,128)}, u32[]{:S(2)}) copy-start(f32[1024,256]{1,0:T(8,128)} %param.9) | copy-start | bytes 3145732
  629.8 93.0 %collective-permute-start.3 = (f32[4096,256]{1,0:T(8,128)S(1)}, f32[4096,256]{1,0:T(8,128)}, u32[]{:S(2)}, u32[]{:S(2)}) collective-permute-start(f32[4096,256]{1,0:T(8,128)S(1)} %add_multiply_fusion), channel_id=1, source_target_pairs={{0,16},{8,24},{16,0},{24,8},{32,48},{40,56},{48,32},{56,40},{64,80... | collective-permute-start | bytes 12582920 | tf_op jit(solution)/shard_map/ppermute | solution.py:16
Sparse Core Ops, SparseCore 0:
  722.9 125.2 reduce-scatter.1
